TPU v7x, 32 devices: a whole 2x2x4 slice. The times are simulated.
32 devices in a mesh: seqb: 4 (over x, core), seqt: 2 (over y), ch: 4 (over z).
Axes of the slice: x: 2, y: 2, z: 4, core: 2. Of those that a mesh axis runs over, the one named last changes fastest.
Arguments:
- query_gate: bfloat16 [2048, 4096], P(('seqb', 'seqt'), 'ch'), may hold values from -6 to 6
- key_proj: bfloat16 [2048, 4096], P(('seqb', 'seqt'), 'ch'), may hold values from -6 to 6
- value_proj: bfloat16 [2048, 4096], P(('seqb', 'seqt'), 'ch'), may hold values from -6 to 6
- filters: float32 [2048, 4096], P(('seqb', 'seqt'), 'ch'), may hold values from -4 to 4
- skip_gain: float32 [4096], P('ch'), may hold values from 0.5 to 2
- w_out: bfloat16 [4096, 4096], P('ch', ('seqb', 'seqt')), may hold values from -0.09375 to 0.09375
Outputs:
- layer_out: bfloat16 [2048, 4096], P(('seqb', 'seqt'), 'ch')
All inputs are finite; a program needn't handle non-finite values.
Results may differ from a plain program's by a relative error of at most 0.0049.
Values may be sent and summed in bfloat16 or wider, within the bound.
A program may use at most 128 MiB of HBM per device.

v0:
```python
import math

import jax
import jax.numpy as jnp
from jax import lax
from jax.sharding import PartitionSpec as P

TWO_PI = 2.0 * math.pi


def unit_angle(numer, denom):
    return TWO_PI * (numer % denom).astype(jnp.float32) / denom


def regroup(blocks):
    return lax.all_to_all(blocks, ("seqb", "seqt"), split_axis=0, concat_axis=0, tiled=True)


def spread_convolve(product, filters):
    highest = lax.Precision.HIGHEST
    rows_here, width = product.shape
    seq_devices = lax.axis_size(("seqb", "seqt"))
    share = rows_here // seq_devices
    period = 2 * seq_devices * rows_here
    position = lax.axis_index(("seqb", "seqt"))
    stacked = jnp.stack(
        [product.reshape(seq_devices, share, width), filters.reshape(seq_devices, share, width)],
        axis=1,
    )
    columns = regroup(stacked)
    freq_index = jnp.arange(2 * seq_devices, dtype=jnp.int32)[:, None, None]
    block_index = jnp.arange(seq_devices, dtype=jnp.int32)[None, None, :]
    local_index = position * share + jnp.arange(share, dtype=jnp.int32)[None, :, None]
    angle_one = unit_angle(freq_index * (block_index * rows_here + local_index), period)
    kernel_one = jnp.stack([jnp.cos(angle_one), -jnp.sin(angle_one)], axis=1)
    first_section = jnp.einsum("aekr,rskc->aeskc", kernel_one, columns, precision=highest)
    first_section = first_section.reshape(seq_devices, 2, 2, 2, share, width)
    mixed = regroup(first_section)
    token_index = (
        jnp.arange(seq_devices, dtype=jnp.int32)[None, :, None] * share
        + jnp.arange(share, dtype=jnp.int32)[None, None, :]
    )
    bin_index = jnp.arange(rows_here, dtype=jnp.int32)[:, None, None]
    angle_two = unit_angle(token_index * bin_index, rows_here)
    cosine_two = jnp.cos(angle_two)
    sine_two = jnp.sin(angle_two)
    kernel_two = jnp.stack(
        [jnp.stack([cosine_two, sine_two], axis=2), jnp.stack([-sine_two, cosine_two], axis=2)],
        axis=1,
    )
    spectra = jnp.einsum("bfpek,pgeskc->gsfbc", kernel_two, mixed, precision=highest)
    signal_re = spectra[:, 0, 0]
    signal_im = spectra[:, 0, 1]
    filter_re = spectra[:, 1, 0]
    filter_im = spectra[:, 1, 1]
    response = jnp.stack(
        [
            signal_re * filter_re - signal_im * filter_im,
            signal_re * filter_im + signal_im * filter_re,
        ],
        axis=1,
    )
    back_token = (
        jnp.arange(seq_devices, dtype=jnp.int32)[:, None, None, None] * share
        + jnp.arange(share, dtype=jnp.int32)[None, :, None, None]
    )
    back_freq = (
        2 * position
        + jnp.arange(2, dtype=jnp.int32)[None, None, :, None]
        + 2 * seq_devices * jnp.arange(rows_here, dtype=jnp.int32)[None, None, None, :]
    )
    angle_three = unit_angle(back_token * back_freq, period)
    cosine_three = jnp.cos(angle_three)
    sine_three = jnp.sin(angle_three)
    kernel_three = jnp.stack(
        [
            jnp.stack([cosine_three, -sine_three], axis=3),
            jnp.stack([sine_three, cosine_three], axis=3),
        ],
        axis=3,
    )
    inverse_section = jnp.einsum("pkgfeb,gebc->pgfkc", kernel_three, response, precision=highest)
    by_frequency = regroup(inverse_section)
    out_block = jnp.arange(seq_devices, dtype=jnp.int32)[:, None, None]
    freq_block = (
        2 * jnp.arange(seq_devices, dtype=jnp.int32)[None, :, None]
        + jnp.arange(2, dtype=jnp.int32)[None, None, :]
    )
    angle_four = unit_angle(out_block * freq_block, 2 * seq_devices)
    kernel_four = jnp.stack([jnp.cos(angle_four), -jnp.sin(angle_four)], axis=3) / period
    spatial = jnp.einsum("rpgf,pgfkc->rkc", kernel_four, by_frequency, precision=highest)
    return regroup(spatial).reshape(rows_here, width)


def shards(query_gate, key_proj, value_proj, filters, skip_gain, w_out):
    product = key_proj.astype(jnp.float32) * value_proj.astype(jnp.float32)
    convolved = spread_convolve(product, filters)
    gated_rows = (
        query_gate.astype(jnp.float32) * (convolved + skip_gain[None, :] * product)
    ).astype(jnp.bfloat16)
    partial_sums = jnp.dot(
        gated_rows,
        lax.all_gather(w_out, ("seqb", "seqt"), axis=1, tiled=True),
        preferred_element_type=jnp.float32,
    )
    return lax.psum_scatter(partial_sums, "ch", scatter_dimension=1, tiled=True).astype(
        jnp.bfloat16
    )


def solution(mesh):
    return jax.shard_map(
        shards,
        mesh=mesh,
        in_specs=(
            P(("seqb", "seqt"), "ch"),
            P(("seqb", "seqt"), "ch"),
            P(("seqb", "seqt"), "ch"),
            P(("seqb", "seqt"), "ch"),
            P("ch"),
            P("ch", ("seqb", "seqt")),
        ),
        out_specs=P(("seqb", "seqt"), "ch"),
        check_vma=False,
    )
```

profile of v0, /device:TPU:13, one launch (start us, length us, event | category | flops | bytes accessed | tf_op | source)
XLA Modules:
  0.0 395.6 jit_solution(5716657834314799712)
XLA Ops:
  6.5 1.4 convert_multiply_fusion
  7.9 1.4 pad_maximum_fusion
  9.3 3.0 copy.24
  12.3 5.0 %all-to-all-start = ((f32[8,2,32,1024]{3,1,2,0:T(2,128)}), f32[8,2,32,1024]{3,1,2,0:T(2,128)S(1)}, u32[]{:S(2)}, u32[]{:S(2)}) async-start(f32[8,2,32,1024]{3,1,2,0:T(2,128)} %copy.24), calls=%async_computation | async-start | bytes 4194304 | tf_op jit(solution)/shard_map/all_to_all | solution.py:16
  17.4 0.1 broadcast_add_fusion
  17.5 0.6 fusion.45
  18.1 23.5 %all-to-all-done = f32[8,2,32,1024]{3,1,2,0:T(2,128)S(1)} async-done(((f32[8,2,32,1024]{3,1,2,0:T(2,128)}), f32[8,2,32,1024]{3,1,2,0:T(2,128)S(1)}, u32[]{:S(2)}, u32[]{:S(2)}) %all-to-all-start) | async-done | bytes 2097184 | tf_op jit(solution)/shard_map/all_to_all | solution.py:16
  41.6 7.4 %convolution_bitcast_fusion = f32[16,2,2,32,1024]{4,0,1,2,3:T(8,128)S(1)} fusion(f32[8,2,32,1024,1]{3,1,2,0,4:T(2,128)S(1)} %bitcast.86, f32[16,1,32,8]{0,3,1,2:T(8,128)S(1)} %get-tuple-element.13, f32[16,1,32,8]{0,3,1,2:T(8,128)S(1)} %get-tuple-element.12), kind=kOutput, calls=%fused_computation.8 | convolution fusion | flops 201334784 | bytes 10518528 | tf_op jit(solution)/shard_map/aekr,rskc->aeskc/dot_general | solution.py:36
  49.0 8.3 %copy.51 = f32[16,2,2,32,1024]{4,3,1,2,0:T(8,128)} copy(f32[16,2,2,32,1024]{4,0,1,2,3:T(8,128)S(1)} %convolution_bitcast_fusion) | data formatting | bytes 16777216 | tf_op jit(solution)/shard_map/reshape | solution.py:37
  57.3 6.0 %all-to-all-start.1 = ((f32[8,2,2,2,32,1024]{5,4,2,3,1,0:T(8,128)}), f32[8,2,2,2,32,1024]{5,4,2,3,1,0:T(8,128)}, u32[]{:S(2)}, u32[]{:S(2)}) async-start(f32[8,2,2,2,32,1024]{5,4,2,3,1,0:T(8,128)} %bitcast.83), calls=%async_computation.1 | async-start | bytes 16777216 | tf_op jit(solution)/shard_map/all_to_all | solution.py:16
  63.2 0.0 all-gather.2.cloned.1.call-start
  63.2 0.7 all-gather.2.cloned.1.call-update
  64.0 0.1 iota_add_fusion
  64.0 0.1 copy.34
  64.1 1.1 fusion.39
  65.2 0.1 maximum_bitcast_fusion.4
  65.4 0.1 broadcast_add_fusion.1
  65.4 2.1 fusion.35
  67.6 0.2 maximum_bitcast_fusion.2
  67.7 121.4 %all-to-all-done.1 = f32[8,2,2,2,32,1024]{5,4,2,3,1,0:T(8,128)} async-done(((f32[8,2,2,2,32,1024]{5,4,2,3,1,0:T(8,128)}), f32[8,2,2,2,32,1024]{5,4,2,3,1,0:T(8,128)}, u32[]{:S(2)}, u32[]{:S(2)}) %all-to-all-start.1) | async-done | bytes 8388640 | tf_op jit(solution)/shard_map/all_to_all | solution.py:16
  189.1 15.7 %fusion = f32[2,2,1024,256,2,1,1]{3,2,5,0,4,1,6:T(8,128)S(1)} fusion(f32[8,2,2,2,32,1024]{5,4,2,3,1,0:T(8,128)} %all-to-all-done.1, f32[256,1,8,2,32]{0,4,2,3,1:T(8,128)S(1)} %get-tuple-element.8, f32[256,1,8,2,32]{0,4,2,3,1:T(8,128)S(1)} %get-tuple-element.7), kind=kOutput, calls=%fused_computation | convolution fusion | flops 12885164032 | bytes 17825792 | tf_op jit(solution)/shard_map/bfpek,pgeskc->gsfbc/dot_general | solution.py:51
  204.8 0.5 copy.74
  205.4 0.5 fusion.14
  205.9 0.5 fusion.12
  206.5 7.3 %fusion.6 = f32[8,2,2,32,1024]{4,0,1,2,3:T(8,128)S(1)} fusion(f32[8,32,2,1,2,256]{5,0,4,2,3,1:T(8,128)S(1)} %get-tuple-element.6, f32[8,32,2,1,2,256]{5,0,4,2,3,1:T(8,128)S(1)} %get-tuple-element.5, f32[2,1,256,1024]{2,3,0,1:T(8,128)S(1)} %fusion.12, f32[2,1,256,1024]{2,3,0,1:T(8,128)S(1)} %fusion.14), kind=kOutput, calls=%fused_computation.9 | convolution fusion | flops 6444023808 | bytes 10485760 | tf_op jit(solution)/shard_map/pkgfeb,gebc->pgfkc/dot_general | solution.py:82
  213.8 5.4 %copy.37 = f32[8,2,2,32,1024]{4,1,2,3,0:T(2,128)} copy(f32[8,2,2,32,1024]{4,0,1,2,3:T(8,128)S(1)} %fusion.6) | data formatting | bytes 8388608 | tf_op jit(solution)/shard_map/pkgfeb,gebc->pgfkc/transpose | solution.py:82
  219.2 5.5 %all-to-all-start.2 = ((f32[8,2,2,32,1024]{4,1,2,3,0:T(2,128)}), f32[8,2,2,32,1024]{4,1,2,3,0:T(2,128)}, u32[]{:S(2)}, u32[]{:S(2)}) async-start(f32[8,2,2,32,1024]{4,1,2,3,0:T(2,128)} %copy.37), calls=%async_computation.2 | async-start | bytes 8388608 | tf_op jit(solution)/shard_map/all_to_all | solution.py:16
  224.7 0.0 reduce-scatter.2.cloned.1.call-start
  224.7 0.1 fusion.57
  224.8 47.2 %all-to-all-done.2 = f32[8,2,2,32,1024]{4,1,2,3,0:T(2,128)} async-done(((f32[8,2,2,32,1024]{4,1,2,3,0:T(2,128)}), f32[8,2,2,32,1024]{4,1,2,3,0:T(2,128)}, u32[]{:S(2)}, u32[]{:S(2)}) %all-to-all-start.2) | async-done | bytes 4194336 | tf_op jit(solution)/shard_map/all_to_all | solution.py:16
  272.0 0.0 copy-start
  272.0 0.0 copy-start.1
  272.0 0.0 copy-start.2
  272.0 0.0 copy-start.3
  272.0 11.3 %fusion.16 = f32[8,32,1024]{2,0,1:T(8,128)S(1)} fusion(f32[8,2,2,32,1024]{4,1,2,3,0:T(2,128)} %all-to-all-done.2, f32[8,8,2,1]{1,0,2,3:T(8,128)S(1)} %get-tuple-element.18, f32[8,8,2,1]{1,0,2,3:T(8,128)S(1)} %get-tuple-element.17), kind=kOutput, calls=%fused_computation.21 | convolution fusion | flops 100663808 | bytes 5243904 | tf_op jit(solution)/shard_map/rpgf,pgfkc->rkc/dot_general | solution.py:91
  283.3 0.6 copy.39
  284.0 17.0 %all_to_all.20 = f32[8,32,1024]{2,1,0:T(8,128)S(1)} all-to-all(f32[8,32,1024]{2,1,0:T(8,128)S(1)} %copy.39), channel_id=1, replica_groups=mesh['seqb'=4,'seqt'=2,'ch'=4] {'seqb','seqt'}, dimensions={0} | all-to-all | bytes 2097152 | tf_op jit(solution)/shard_map/all_to_all | solution.py:16
  301.0 0.0 copy-done
  301.0 0.0 copy-done.1
  301.0 0.0 copy-done.2
  301.0 0.0 copy-done.3
  301.0 0.3 fusion.20
  301.3 0.0 all-gather.2.cloned.1.call-done
  301.3 7.7 %fusion.62 = f32[256,4096]{1,0:T(8,128)} fusion(bf16[256,1024]{1,0:T(8,128)(2,1)S(1)} %fusion.20, bf16[1024,4096]{1,0:T(8,128)(2,1)} %all-gather.2.cloned.1.call-done), kind=kOutput, calls=%fused_computation.99 | convolution fusion | flops 2147483648 | bytes 13107200 | tf_op jit(solution)/shard_map/dot_general | solution.py:101
  309.0 0.0 reduce-scatter.2.cloned.1.call-update
  309.1 77.3 %reduce-scatter.2.cloned.1.call-done = f32[256,1024]{1,0:T(8,128)} async-done(((f32[256,4096]{1,0:T(8,128)}), f32[256,1024]{1,0:T(8,128)}) %reduce-scatter.2.cloned.1.call-update) | async-done | bytes 1048592 | tf_op jit(solution)/shard_map/reduce_scatter | solution.py:106
  386.4 2.1 convert_element_type.95
  (7 shorter events, 0.0 us)
Async XLA Ops:
  12.3 29.3 %all-to-all-start = ((f32[8,2,32,1024]{3,1,2,0:T(2,128)}), f32[8,2,32,1024]{3,1,2,0:T(2,128)S(1)}, u32[]{:S(2)}, u32[]{:S(2)}) async-start(f32[8,2,32,1024]{3,1,2,0:T(2,128)} %copy.24), calls=%async_computation | async-start | bytes 4194304 | tf_op jit(solution)/shard_map/all_to_all | solution.py:16
  57.3 131.9 %all-to-all-start.1 = ((f32[8,2,2,2,32,1024]{5,4,2,3,1,0:T(8,128)}), f32[8,2,2,2,32,1024]{5,4,2,3,1,0:T(8,128)}, u32[]{:S(2)}, u32[]{:S(2)}) async-start(f32[8,2,2,2,32,1024]{5,4,2,3,1,0:T(8,128)} %bitcast.83), calls=%async_computation.1 | async-start | bytes 16777216 | tf_op jit(solution)/shard_map/all_to_all | solution.py:16
  63.2 238.1 %all-gather.2.cloned.1.call-start = ((), (), s32[]{:S(2)}) async-start(), calls=%async_computation.5 | async-start | bytes 9437184 | tf_op jit(solution)/shard_map/all_gather | solution.py:103
  219.2 52.9 %all-to-all-start.2 = ((f32[8,2,2,32,1024]{4,1,2,3,0:T(2,128)}), f32[8,2,2,32,1024]{4,1,2,3,0:T(2,128)}, u32[]{:S(2)}, u32[]{:S(2)}) async-start(f32[8,2,2,32,1024]{4,1,2,3,0:T(2,128)} %copy.37), calls=%async_computation.2 | async-start | bytes 8388608 | tf_op jit(solution)/shard_map/all_to_all | solution.py:16
  224.7 161.7 %reduce-scatter.2.cloned.1.call-start = ((), (), s32[]{:S(2)}) async-start(), calls=%async_computation.6 | async-start | bytes 5242880 | tf_op jit(solution)/shard_map/reduce_scatter | solution.py:106
  272.0 28.9 %copy-start = (bf16[256,1024]{1,0:T(8,128)(2,1)S(1)}, bf16[256,1024]{1,0:T(8,128)(2,1)}, u32[]{:S(2)}) copy-start(bf16[256,1024]{1,0:T(8,128)(2,1)} %param.8) | copy-start | bytes 1572868
  272.0 28.9 %copy-start.1 = (bf16[256,1024]{1,0:T(8,128)(2,1)S(1)}, bf16[256,1024]{1,0:T(8,128)(2,1)}, u32[]{:S(2)}) copy-start(bf16[256,1024]{1,0:T(8,128)(2,1)} %param.7) | copy-start | bytes 1572868
  272.0 28.9 %copy-start.2 = (bf16[256,1024]{1,0:T(8,128)(2,1)S(1)}, bf16[256,1024]{1,0:T(8,128)(2,1)}, u32[]{:S(2)}) copy-start(bf16[256,1024]{1,0:T(8,128)(2,1)} %param.6) | copy-start | bytes 1572868
  272.0 28.9 %copy-start.3 = (f32[1024]{0:T(1024)S(1)}, f32[1024]{0:T(1024)}, u32[]{:S(2)}) copy-start(f32[1024]{0:T(1024)} %param.10) | copy-start | bytes 12292
Sparse Core Ops, SparseCore 0:
  65.9 123.2 all-gather.1
  309.2 77.1 reduce-scatter.1
where the time goes:
time: 400 us; the launch traced here: 396 us
  waiting for transfers between devices  270 us (68%)
  matrix products  49.4 us (12%)
  local copies, waits for them, and re-layouts  17.9 us (4%)
  blocking collectives  17 us (4%)
  starting transfers between devices  16.6 us (4%)
  between operations  13.8 us (3%)
  other arithmetic  10.7 us (3%)
    all_to_all x3, waiting for transfers between devices, regroup(): lax.all_to_all(blocks, ('seqb', 'seqt'), split_axis=0, concat_axis=0, til...  192 us
    reduce_scatter x1, waiting for transfers between devices, shards(): lax.psum_scatter(partial_sums, 'ch', scatter_dimension=1, tiled=True)  77.3 us
    all_to_all x1, blocking collectives, regroup(): lax.all_to_all(blocks, ('seqb', 'seqt'), split_axis=0, concat_axis=0, til...  17 us
    all_to_all x3, starting transfers between devices, regroup(): lax.all_to_all(blocks, ('seqb', 'seqt'), split_axis=0, concat_axis=0, til...  16.6 us
    dot_general x1, matrix products, spread_convolve(): jnp.einsum('bfpek,pgeskc->gsfbc', kernel_two, mixed, precision=highest)  15.7 us
    dot_general x1, matrix products, spread_convolve(): jnp.einsum('rpgf,pgfkc->rkc', kernel_four, by_frequency, precision=highest)  11.3 us
    reshape x1, local copies, waits for them, and re-layouts, spread_convolve(): first_section = first_section.reshape(seq_devices, 2, 2, 2, share, width)  8.26 us
  transfers between devices with their start and end apart: 5, of which 4 were waited for; matrix products, arithmetic and copies ran while one was open for 12% of the time, Pallas kernels for 0%

commit v1 on v0

v1 whole, which is shorter than its diff:
```python
import numpy as np

import jax
import jax.numpy as jnp
from jax import lax
from jax.experimental import pallas as pl
from jax.experimental.pallas import tpu as pltpu
from jax.sharding import PartitionSpec as P

SEQ = ("seqb", "seqt")


def split(x):
    hi = x.astype(jnp.bfloat16)
    return hi, (x - hi.astype(jnp.float32)).astype(jnp.bfloat16)


def dot32(m_hi, m_lo, a):
    a_hi, a_lo = split(a)
    dot = lambda p, q: jnp.dot(p, q, preferred_element_type=jnp.float32)
    return dot(m_hi, a_hi) + dot(m_lo, a_hi) + dot(m_hi, a_lo)


def conv_kernel(coef_ref, x_ref, base_ref, twid_ref, out_ref, acc_ref):
    blocks, rows, both = x_ref.shape
    width = both // 2
    k = pl.program_id(0)

    @pl.when(k == 0)
    def _():
        acc_ref[...] = jnp.zeros_like(acc_ref)

    re = jnp.zeros((rows, both), jnp.float32)
    im = jnp.zeros((rows, both), jnp.float32)
    for n in range(blocks):
        x = x_ref[n].astype(jnp.float32)
        re += coef_ref[0, k, n] * x
        im -= coef_ref[1, k, n] * x
    tc = twid_ref[0, :, 0:1]
    ts = twid_ref[0, :, 1:2]
    a = jnp.concatenate([re * tc + im * ts, im * tc - re * ts], axis=1)
    p = dot32(base_ref[0], base_ref[1], a)
    q = dot32(base_ref[2], base_ref[3], a)
    br = p[:, :both] + q[:, both:]
    bi = p[:, both:] - q[:, :both]
    sr, fr = br[:, :width], br[:, width:]
    si, fi = bi[:, :width], bi[:, width:]
    y = jnp.concatenate([sr * fr - si * fi, sr * fi + si * fr], axis=1)
    p = dot32(base_ref[0], base_ref[1], y)
    q = dot32(base_ref[2], base_ref[3], y)
    zr = p[:, :width] - q[:, width:]
    zi = p[:, width:] + q[:, :width]
    vr = zr * tc - zi * ts
    vi = zi * tc + zr * ts
    for n in range(blocks):
        acc_ref[n] += coef_ref[2, k, n] * vr - coef_ref[3, k, n] * vi

    @pl.when(k == blocks)
    def _():
        out_ref[...] = acc_ref[...].astype(out_ref.dtype)


def tables(blocks, rows):
    period = 2 * blocks * rows
    k = np.arange(blocks + 1)
    n = np.arange(blocks)
    ang = 2 * np.pi * ((k[:, None] * n[None, :]) % (2 * blocks)) / (2 * blocks)
    gain = np.where((k == 0) | (k == blocks), 1.0, 2.0)[:, None] / period
    coef = np.stack([np.cos(ang), np.sin(ang), gain * np.cos(ang), gain * np.sin(ang)])
    r = np.arange(rows)
    ang = 2 * np.pi * ((r[:, None] * r[None, :]) % rows) / rows
    parts = []
    for m in (np.cos(ang), np.sin(ang)):
        hi = m.astype(jnp.bfloat16)
        parts += [hi, (m - hi.astype(np.float64)).astype(jnp.bfloat16)]
    ang = 2 * np.pi * ((k[:, None] * r[None, :]) % period) / period
    twid = np.stack([np.cos(ang), np.sin(ang)], axis=-1)
    return coef.astype(np.float32), np.stack(parts), twid.astype(np.float32)


def convolve(columns):
    blocks, rows, both = columns.shape
    coef, base, twid = tables(blocks, rows)
    return pl.pallas_call(
        conv_kernel,
        grid=(blocks + 1,),
        out_shape=jax.ShapeDtypeStruct((blocks, rows, both // 2), jnp.bfloat16),
        in_specs=[
            pl.BlockSpec(memory_space=pltpu.SMEM),
            pl.BlockSpec((blocks, rows, both), lambda k: (0, 0, 0)),
            pl.BlockSpec((4, rows, rows), lambda k: (0, 0, 0)),
            pl.BlockSpec((1, rows, 2), lambda k: (k, 0, 0)),
        ],
        out_specs=pl.BlockSpec((blocks, rows, both // 2), lambda k: (0, 0, 0)),
        scratch_shapes=[pltpu.VMEM((blocks, rows, both // 2), jnp.float32)],
        compiler_params=pltpu.CompilerParams(vmem_limit_bytes=48 * 1024 * 1024),
        cost_estimate=pl.CostEstimate(
            flops=36 * (blocks + 1) * rows * rows * both, bytes_accessed=4 * 1024 * 1024, transcendentals=0
        ),
    )(jnp.asarray(coef), columns, jnp.asarray(base), jnp.asarray(twid))


def shards(query_gate, key_proj, value_proj, filters, skip_gain, w_out):
    rows, channels = key_proj.shape
    seq = lax.axis_size(SEQ)
    width = channels // seq
    product = key_proj.astype(jnp.float32) * value_proj.astype(jnp.float32)
    pieces = lambda a: a.astype(jnp.bfloat16).reshape(rows, seq, width).transpose(1, 0, 2)
    stacked = jnp.concatenate([pieces(product), pieces(filters)], axis=2)
    columns = lax.all_to_all(stacked, SEQ, split_axis=0, concat_axis=0, tiled=True)
    spatial = lax.all_to_all(convolve(columns), SEQ, split_axis=0, concat_axis=0, tiled=True)
    convolved = spatial.transpose(1, 0, 2).reshape(rows, channels).astype(jnp.float32)
    gated_rows = (
        query_gate.astype(jnp.float32) * (convolved + skip_gain[None, :] * product)
    ).astype(jnp.bfloat16)
    weights = lax.all_gather(w_out, SEQ, axis=1, tiled=True)
    partial_sums = jnp.dot(gated_rows, weights, preferred_element_type=jnp.float32)
    return lax.psum_scatter(partial_sums, "ch", scatter_dimension=1, tiled=True).astype(
        jnp.bfloat16
    )


def solution(mesh):
    return jax.shard_map(
        shards,
        mesh=mesh,
        in_specs=(
            P(SEQ, "ch"),
            P(SEQ, "ch"),
            P(SEQ, "ch"),
            P(SEQ, "ch"),
            P("ch"),
            P("ch", SEQ),
        ),
        out_specs=P(SEQ, "ch"),
        check_vma=False,
    )
```

time: 400 us -> 179 us (0.45)
  waiting for transfers between devices: 270 us -> 91.9 us
  matrix products: 49.4 us -> 7.73 us
  Pallas kernels: 0 us -> 18.4 us
  starting transfers between devices: 16.6 us -> 4.18 us
  blocking collectives: 17 us -> 28.8 us
  local copies, waits for them, and re-layouts: 17.9 us -> 7.37 us
  other arithmetic: 10.7 us -> 5.06 us
    all_to_all x3 -> x1, waiting for transfers between devices: 192 us -> 12.6 us  [shards(): lax.all_to_all(convolve(columns), SEQ, split_axis=0, concat_axis=0, tiled...]
    dot_general x5 -> x1, matrix products: 49.4 us -> 7.73 us  [shards(): jnp.dot(gated_rows, weights, preferred_element_type=jnp.float32)]
    pallas_call x0 -> x1, Pallas kernels: none -> 18.4 us  [convolve(): pl.pallas_call(conv_kernel, grid=(blocks + 1,), out_shape=jax.ShapeDtypeS...]
    all_to_all x3 -> x1, starting transfers between devices: 16.6 us -> 4.18 us  [shards(): lax.all_to_all(convolve(columns), SEQ, split_axis=0, concat_axis=0, tiled...]
    all_to_all x1, blocking collectives: 17 us -> 28.8 us  [shards(): lax.all_to_all(stacked, SEQ, split_axis=0, concat_axis=0, tiled=True)]
    reshape x1 -> x2, local copies, waits for them, and re-layouts: 8.26 us -> 2.05 us  [shards(): a.astype(jnp.bfloat16).reshape(rows, seq, width).transpose(1, 0, 2)]
    transpose x1 -> x0, local copies, waits for them, and re-layouts: 5.41 us -> none  [spread_convolve(): jnp.einsum('pkgfeb,gebc->pgfkc', kernel_three, response, precision=highest)]
    unnamed x8 -> x14, local copies, waits for them, and re-layouts: 0.01 us -> 4.99 us
  transfers between devices with their start and end apart: 5 -> 3, of which waited for: 4 -> 3; matrix products, arithmetic and copies ran while one was open for 12% -> 6% of each run, Pallas kernels for 0% -> 10%
where the time goes in v1:
time: 179 us; the launch traced here: 177 us
  waiting for transfers between devices  91.9 us (51%)
  blocking collectives  28.8 us (16%)
  Pallas kernels  18.4 us (10%)
  between operations  13.5 us (8%)
  matrix products  7.73 us (4%)
  local copies, waits for them, and re-layouts  7.37 us (4%)
  other arithmetic  5.06 us (3%)
  starting transfers between devices  4.18 us (2%)
    reduce_scatter x1, waiting for transfers between devices, shards(): lax.psum_scatter(partial_sums, 'ch', scatter_dimension=1, tiled=True)  77.5 us
    all_to_all x1, blocking collectives, shards(): lax.all_to_all(stacked, SEQ, split_axis=0, concat_axis=0, tiled=True)  28.8 us
    pallas_call x1, Pallas kernels, convolve(): pl.pallas_call(conv_kernel, grid=(blocks + 1,), out_shape=jax.ShapeDtypeS...  18.4 us
    all_to_all x1, waiting for transfers between devices, shards(): lax.all_to_all(convolve(columns), SEQ, split_axis=0, concat_axis=0, tiled...  12.6 us
    dot_general x1, matrix products, shards(): jnp.dot(gated_rows, weights, preferred_element_type=jnp.float32)  7.73 us
    unnamed x14, local copies, waits for them, and re-layouts  4.99 us
    all_to_all x1, starting transfers between devices, shards(): lax.all_to_all(convolve(columns), SEQ, split_axis=0, concat_axis=0, tiled...  4.18 us
  transfers between devices with their start and end apart: 3, of which 3 were waited for; matrix products, arithmetic and copies ran while one was open for 6% of the time, Pallas kernels for 10%

profile of v1, /device:TPU:13, one launch (start us, length us, event | category | flops | bytes accessed | tf_op | source)
XLA Modules:
  0.0 176.8 jit_solution(10289121750779156810)
XLA Ops:
  6.5 0.0 all-gather.2.cloned.1.call-start
  6.5 0.7 all-gather.2.cloned.1.call-update
  7.3 1.2 copy.11
  8.5 1.2 copy.12
  9.8 0.1 fusion.2
  9.9 0.0 copy-start
  9.9 0.0 copy-start.1
  9.9 0.0 copy-start.2
  9.9 1.0 copy.13
  11.0 1.4 copy.14
  12.4 1.0 copy.15
  13.4 1.3 pad_maximum_fusion
  14.7 28.8 %all_to_all.10.x_ref = bf16[8,256,256]{2,1,0:T(8,128)(2,1)S(1)} all-to-all(bf16[8,256,256]{2,1,0:T(8,128)(2,1)S(1)} %pad_maximum_fusion), channel_id=1, replica_groups=mesh['seqb'=4,'seqt'=2,'ch'=4] {'seqb','seqt'}, dimensions={0} | all-to-all | bytes 2097152 | tf_op jit(solution)/shard_map/all_to_all | solution.py:110
  43.5 0.0 copy-done
  43.5 0.0 copy-done.1
  43.5 0.0 copy-done.2
  43.6 0.0 copy-start.3
  43.6 18.4 %shard_map.91 = bf16[8,256,128]{2,1,0:T(8,128)(2,1)} custom-call(f32[4,9,8]{2,1,0:T(8,128)S(1)} %copy-done.2, bf16[8,256,256]{2,1,0:T(8,128)(2,1)S(1)} %all_to_all.10.x_ref, bf16[4,256,256]{2,1,0:T(8,128)(2,1)S(1)} %copy-done.1, f32[9,256,2]{2,1,0:T(8,128)S(1)} %copy-done), custom_call_target="tpu_custom_call" | custom-call | flops 5435817984 | bytes 4194304 | tf_op jit(solution)/shard_map/pallas_call | solution.py:84
  61.9 0.0 copy-start.4
  61.9 4.2 %all-to-all-start.1 = ((bf16[8,256,128]{2,1,0:T(8,128)(2,1)}), bf16[8,256,128]{2,1,0:T(8,128)(2,1)S(1)}, u32[]{:S(2)}, u32[]{:S(2)}) async-start(bf16[8,256,128]{2,1,0:T(8,128)(2,1)} %shard_map.91), calls=%async_computation.1 | async-start | bytes 1048576 | tf_op jit(solution)/shard_map/all_to_all | solution.py:111
  66.1 0.0 reduce-scatter.2.cloned.1.call-start
  66.1 0.0 copy-done.3
  66.1 1.0 copy.10
  67.2 12.6 %all-to-all-done.1 = bf16[8,256,128]{2,1,0:T(8,128)(2,1)S(1)} async-done(((bf16[8,256,128]{2,1,0:T(8,128)(2,1)}), bf16[8,256,128]{2,1,0:T(8,128)(2,1)S(1)}, u32[]{:S(2)}, u32[]{:S(2)}) %all-to-all-start.1) | async-done | bytes 524320 | tf_op jit(solution)/shard_map/all_to_all | solution.py:111
  79.7 0.1 convert_bitcast_fusion
  79.8 0.3 copy.16
  80.1 0.0 copy-done.4
  80.1 1.4 fusion.1
  81.6 1.1 all-gather.2.cloned.1.call-done
  82.7 7.7 %fusion.3 = f32[256,4096]{1,0:T(8,128)} fusion(bf16[256,1024]{0,1:T(8,128)(2,1)S(1)} %fusion.1, bf16[1024,4096]{1,0:T(8,128)(2,1)} %all-gather.2.cloned.1.call-done), kind=kOutput, calls=%fused_computation.7 | convolution fusion | flops 2147483648 | bytes 13107200 | tf_op jit(solution)/shard_map/dot_general | solution.py:117
  90.4 0.0 reduce-scatter.2.cloned.1.call-update
  90.4 77.5 %reduce-scatter.2.cloned.1.call-done = f32[256,1024]{1,0:T(8,128)} async-done(((f32[256,4096]{1,0:T(8,128)}), f32[256,1024]{1,0:T(8,128)}) %reduce-scatter.2.cloned.1.call-update) | async-done | bytes 1048592 | tf_op jit(solution)/shard_map/reduce_scatter | solution.py:118
  167.9 2.1 %convert_element_type.39 = bf16[256,1024]{1,0:T(8,128)(2,1)} convert(f32[256,1024]{1,0:T(8,128)} %reduce-scatter.2.cloned.1.call-done) | non-fusion elementwise | flops 262144 | bytes 1572864 | tf_op jit(solution)/shard_map/convert_element_type | solution.py:118
Async XLA Ops:
  6.5 76.2 %all-gather.2.cloned.1.call-start = ((), (), s32[]{:S(2)}) async-start(), calls=%async_computation.3 | async-start | bytes 9437184 | tf_op jit(solution)/shard_map/all_gather | solution.py:116
  9.9 33.6 %copy-start = (f32[9,256,2]{2,1,0:T(8,128)S(1)}, f32[9,256,2]{2,1,0:T(8,128)}, u32[]{:S(2)}) copy-start(f32[9,256,2]{2,1,0:T(8,128)} %constant.8.clone.twid_ref) | copy-start | bytes 55300
  9.9 33.6 %copy-start.1 = (bf16[4,256,256]{2,1,0:T(8,128)(2,1)S(1)}, bf16[4,256,256]{2,1,0:T(8,128)(2,1)}, u32[]{:S(2)}) copy-start(bf16[4,256,256]{2,1,0:T(8,128)(2,1)} %constant.7.clone.base_ref) | copy-start | bytes 1572868
  9.9 33.6 %copy-start.2 = (f32[4,9,8]{2,1,0:T(8,128)S(1)}, f32[4,9,8]{2,1,0:T(8,128)}, u32[]{:S(2)}) copy-start(f32[4,9,8]{2,1,0:T(8,128)} %constant.6.clone.coef_ref) | copy-start | bytes 3460
  43.6 22.6 %copy-start.3 = (bf16[256,1024]{1,0:T(8,128)(2,1)S(1)}, bf16[256,1024]{1,0:T(8,128)(2,1)}, u32[]{:S(2)}) copy-start(bf16[256,1024]{1,0:T(8,128)(2,1)} %param.9) | copy-start | bytes 1572868
  61.9 18.2 %copy-start.4 = (f32[1024]{0:T(1024)S(1)}, f32[1024]{0:T(1024)}, u32[]{:S(2)}) copy-start(f32[1024]{0:T(1024)} %param.13) | copy-start | bytes 12292
  61.9 17.8 %all-to-all-start.1 = ((bf16[8,256,128]{2,1,0:T(8,128)(2,1)}), bf16[8,256,128]{2,1,0:T(8,128)(2,1)S(1)}, u32[]{:S(2)}, u32[]{:S(2)}) async-start(bf16[8,256,128]{2,1,0:T(8,128)(2,1)} %shard_map.91), calls=%async_computation.1 | async-start | bytes 1048576 | tf_op jit(solution)/shard_map/all_to_all | solution.py:111
  66.1 101.8 %reduce-scatter.2.cloned.1.call-start = ((), (), s32[]{:S(2)}) async-start(), calls=%async_computation.4 | async-start | bytes 5242880 | tf_op jit(solution)/shard_map/reduce_scatter | solution.py:118
Sparse Core Ops, SparseCore 0:
  9.2 73.4 all-gather.1
  90.6 77.2 reduce-scatter.1

commit v2 on v1

--- a/solution.py
+++ b/solution.py
@@ -100,10 +100,231 @@
     )(jnp.asarray(coef), columns, jnp.asarray(base), jnp.asarray(twid))
 
 
+MESH = pl.DeviceIdType.MESH
+
+
+def layer_kernel(coef_ref, q_ref, k_ref, v_ref, f_ref, skip_ref, w_ref, base_ref, twid_ref, out_ref,
+                 xs_send, xs_recv, acc_ref, cs_send, cs_recv, g_ref, w_all, p_send, p_recv, p_own,
+                 o_send, o_recv, in_s, in_r, back_s, back_r, w_s, w_r, g_s, g_r, p_s, p_r, o_s, o_r, local_sem):
+    seq_t = lax.axis_size("seqt")
+    blocks = lax.axis_size("seqb") * seq_t
+    depth = lax.axis_size("ch")
+    ib, it, z = lax.axis_index("seqb"), lax.axis_index("seqt"), lax.axis_index("ch")
+    me = ib * seq_t + it
+    core = ib % 2
+    rows, channels = k_ref.shape
+    width = channels // blocks
+    both = 2 * width
+    cols = w_ref.shape[1]
+    per = blocks // depth
+    place = lambda s: {"seqb": s // seq_t, "seqt": s % seq_t}
+    sibling = {"seqb": ib + 1 - 2 * core}
+
+    def remote(src, dst, send, recv, where):
+        return pltpu.make_async_remote_copy(
+            src_ref=src, dst_ref=dst, send_sem=send, recv_sem=recv, device_id=where, device_id_type=MESH
+        )
+
+    barrier = pltpu.get_barrier_semaphore()
+    for j in range(1, blocks):
+        pl.semaphore_signal(barrier, inc=1, device_id=place((me + j) % blocks), device_id_type=MESH)
+    for j in range(1, depth):
+        pl.semaphore_signal(barrier, inc=1, device_id={"ch": (z + j) % depth}, device_id_type=MESH)
+
+    def piece(d):
+        lanes = pl.ds(pl.multiple_of(d * width, width), width)
+        p = k_ref[:, lanes].astype(jnp.float32) * v_ref[:, lanes].astype(jnp.float32)
+        return jnp.concatenate([p.astype(jnp.bfloat16), f_ref[:, lanes].astype(jnp.bfloat16)], axis=1)
+
+    for j in range(1, blocks):
+        xs_send[j] = piece((me + j) % blocks)
+    pl.semaphore_wait(barrier, blocks + depth - 2)
+
+    entry = [
+        remote(xs_send.at[j], xs_recv.at[me], in_s.at[j], in_r.at[j], place((me + j) % blocks))
+        for j in range(1, blocks)
+    ]
+    for copy in entry:
+        copy.start()
+    xs_recv[me] = piece(me)
+
+    keep = me % per
+    targets = [
+        ((x * 2 + keep) * seq_t + t, x * seq_t + t)
+        for x in range(blocks // seq_t // 2)
+        for t in range(seq_t)
+    ]
+    weight = [
+        (dest, remote(w_ref, w_all.at[me // per], w_s.at[i], w_r.at[me // per], place(dest)))
+        for dest, i in targets
+    ]
+    local = pltpu.make_async_copy(w_ref, w_all.at[me // per], local_sem)
+    mine = core == keep
+
+    @pl.when(mine)
+    def _():
+        local.start()
+
+    def start_weights():
+        for dest, copy in weight:
+            @pl.when(dest != me)
+            def _():
+                copy.start()
+
+    for copy in entry:
+        copy.wait_recv()
+    start_weights()
+
+    acc_ref[...] = jnp.zeros_like(acc_ref)
+
+    def frequency(k, carry):
+        re = jnp.zeros((rows, both), jnp.float32)
+        im = jnp.zeros((rows, both), jnp.float32)
+        for n in range(blocks):
+            x = xs_recv[n].astype(jnp.float32)
+            re += coef_ref[0, k, n] * x
+            im -= coef_ref[1, k, n] * x
+        tc = twid_ref[k, :, 0:1]
+        ts = twid_ref[k, :, 1:2]
+        a = jnp.concatenate([re * tc + im * ts, im * tc - re * ts], axis=1)
+        p = dot32(base_ref[0], base_ref[1], a)
+        q = dot32(base_ref[2], base_ref[3], a)
+        br = p[:, :both] + q[:, both:]
+        bi = p[:, both:] - q[:, :both]
+        sr, fr = br[:, :width], br[:, width:]
+        si, fi = bi[:, :width], bi[:, width:]
+        y = jnp.concatenate([sr * fr - si * fi, sr * fi + si * fr], axis=1)
+        p = dot32(base_ref[0], base_ref[1], y)
+        q = dot32(base_ref[2], base_ref[3], y)
+        zr = p[:, :width] - q[:, width:]
+        zi = p[:, width:] + q[:, :width]
+        vr = zr * tc - zi * ts
+        vi = zi * tc + zr * ts
+        for n in range(blocks):
+            acc_ref[n] += coef_ref[2, k, n] * vr - coef_ref[3, k, n] * vi
+        return carry
+
+    lax.fori_loop(0, blocks + 1, frequency, 0)
+
+    back = []
+    for j in range(1, blocks):
+        d = (me + j) % blocks
+        cs_send[j] = acc_ref[d].astype(jnp.bfloat16)
+        copy = remote(cs_send.at[j], cs_recv.at[me], back_s.at[j], back_r.at[j], place(d))
+        copy.start()
+        back.append(copy)
+    cs_recv[me] = acc_ref[me].astype(jnp.bfloat16)
+    for copy in back:
+        copy.wait_recv()
+    for d in range(blocks):
+        lanes = slice(d * width, (d + 1) * width)
+        p = k_ref[:, lanes].astype(jnp.float32) * v_ref[:, lanes].astype(jnp.float32)
+        conv = cs_recv[d].astype(jnp.float32)
+        g_ref[core, :, lanes] = (
+            q_ref[:, lanes].astype(jnp.float32) * (conv + skip_ref[:, lanes] * p)
+        ).astype(jnp.bfloat16)
+    swap = remote(g_ref.at[core], g_ref.at[core], g_s, g_r, sibling)
+    swap.start()
+    swap.wait()
+
+    def weight_ready(c):
+        source = c * per + core
+
+        @pl.when(source != me)
+        def _():
+            remote(w_ref, w_all.at[c], w_s.at[0], w_r.at[c], sibling).wait_recv()
+
+        @pl.when(source == me)
+        def _():
+            local.wait()
+
+    def give(j):
+        c = (z + j) % depth
+        return remote(p_send.at[j], p_recv.at[j], p_s.at[j], p_r.at[j], {"ch": c})
+
+    def project(j, carry):
+        c = (z + j) % depth
+        weight_ready(c)
+        for half in range(2):
+            part = jnp.dot(g_ref[half], w_all[c], preferred_element_type=jnp.float32)
+            p_send[j, half] = part.astype(jnp.bfloat16)
+        give(j).start()
+        return carry
+
+    lax.fori_loop(1, depth, project, 0)
+    weight_ready(z)
+    for half in range(2):
+        p_own[half] = jnp.dot(g_ref[half], w_all[z], preferred_element_type=jnp.float32)
+    for j in range(1, depth):
+        give(j).wait_recv()
+
+    def total(half):
+        s = p_own[half]
+        for j in range(1, depth):
+            s += p_recv[j, half].astype(jnp.float32)
+        return s.astype(jnp.bfloat16)
+
+    o_send[...] = total(1 - core)
+    last = remote(o_send, o_recv, o_s, o_r, sibling)
+    last.start()
+    out_ref[:, pl.ds(pl.multiple_of(core * cols, cols), cols)] = total(core)
+    last.wait()
+    out_ref[:, pl.ds(pl.multiple_of((1 - core) * cols, cols), cols)] = o_recv[...]
+
+    for copy in entry + back:
+        copy.wait_send()
+    for dest, copy in weight:
+        @pl.when(dest != me)
+        def _():
+            copy.wait_send()
+    for j in range(1, depth):
+        give(j).wait_send()
+
+
+def fused(query_gate, key_proj, value_proj, filters, skip_gain, w_out):
+    rows, channels = key_proj.shape
+    cols = w_out.shape[1]
+    blocks = lax.axis_size(SEQ)
+    depth = lax.axis_size("ch")
+    width = channels // blocks
+    coef, base, twid = tables(blocks, rows)
+    bf16, f32 = jnp.bfloat16, jnp.float32
+    dma = pltpu.SemaphoreType.DMA
+    return pl.pallas_call(
+        layer_kernel,
+        out_shape=jax.ShapeDtypeStruct((rows, channels), bf16),
+        in_specs=[pl.BlockSpec(memory_space=pltpu.SMEM)] + [pl.BlockSpec(memory_space=pltpu.VMEM)] * 8,
+        out_specs=pl.BlockSpec(memory_space=pltpu.VMEM),
+        scratch_shapes=[
+            pltpu.VMEM((blocks, rows, 2 * width), bf16),
+            pltpu.VMEM((blocks, rows, 2 * width), bf16),
+            pltpu.VMEM((blocks, rows, width), f32),
+            pltpu.VMEM((blocks, rows, width), bf16),
+            pltpu.VMEM((blocks, rows, width), bf16),
+            pltpu.VMEM((2, rows, channels), bf16),
+            pltpu.VMEM((depth,) + w_out.shape, bf16),
+            pltpu.VMEM((depth, 2, rows, cols), bf16),
+            pltpu.VMEM((depth, 2, rows, cols), bf16),
+            pltpu.VMEM((2, rows, cols), f32),
+            pltpu.VMEM((rows, cols), bf16),
+            pltpu.VMEM((rows, cols), bf16),
+            dma((blocks,)), dma((blocks,)), dma((blocks,)), dma((blocks,)),
+            dma((blocks // 2,)), dma((depth,)),
+            dma, dma, dma((depth,)), dma((depth,)), dma, dma, dma,
+        ],
+        compiler_params=pltpu.CompilerParams(
+            collective_id=0, has_side_effects=True, vmem_limit_bytes=56 * 1024 * 1024
+        ),
+    )(jnp.asarray(coef), query_gate, key_proj, value_proj, filters, skip_gain[None, :], w_out,
+      jnp.asarray(base), jnp.asarray(twid))
+
+
 def shards(query_gate, key_proj, value_proj, filters, skip_gain, w_out):
     rows, channels = key_proj.shape
     seq = lax.axis_size(SEQ)
     width = channels // seq
+    if width % 128 == 0 and seq == 2 * lax.axis_size("ch") and lax.axis_size("seqb") % 2 == 0:
+        return fused(query_gate, key_proj, value_proj, filters, skip_gain, w_out)
     product = key_proj.astype(jnp.float32) * value_proj.astype(jnp.float32)
     pieces = lambda a: a.astype(jnp.bfloat16).reshape(rows, seq, width).transpose(1, 0, 2)
     stacked = jnp.concatenate([pieces(product), pieces(filters)], axis=2)

time: 179 us -> 126 us (0.70)
  Pallas kernels: 18.4 us -> 124 us
  waiting for transfers between devices: 91.9 us -> 0 us
  blocking collectives: 28.8 us -> 0 us
  between operations: 13.5 us -> 0.01 us
  matrix products: 7.73 us -> 0 us
  local copies, waits for them, and re-layouts: 7.37 us -> 1.87 us
  other arithmetic: 5.06 us -> 0 us
  starting transfers between devices: 4.18 us -> 0 us
    pallas_call x1, Pallas kernels: 18.4 us -> 124 us  [fused(): pl.pallas_call(layer_kernel, out_shape=jax.ShapeDtypeStruct((rows, channe...]
    reduce_scatter x1 -> x0, waiting for transfers between devices: 77.5 us -> none  [shards(): lax.psum_scatter(partial_sums, 'ch', scatter_dimension=1, tiled=True)]
    all_to_all x1 -> x0, blocking collectives: 28.8 us -> none  [shards(): lax.all_to_all(stacked, SEQ, split_axis=0, concat_axis=0, tiled=True)]
    all_to_all x1 -> x0, waiting for transfers between devices: 12.6 us -> none  [shards(): lax.all_to_all(convolve(columns), SEQ, split_axis=0, concat_axis=0, tiled...]
    dot_general x1 -> x0, matrix products: 7.73 us -> none  [shards(): jnp.dot(gated_rows, weights, preferred_element_type=jnp.float32)]
    all_to_all x1 -> x0, starting transfers between devices: 4.18 us -> none  [shards(): lax.all_to_all(convolve(columns), SEQ, split_axis=0, concat_axis=0, tiled...]
    convert_element_type x4 -> x0, other arithmetic: 3.74 us -> none  [the longest x1 2.09 us: shards(): lax.psum_scatter(partial_sums, 'ch', scatter_dimension=1, tiled=True)]
    unnamed x14 -> x1, local copies, waits for them, and re-layouts: 4.99 us -> 1.87 us
  transfers between devices with their start and end apart: 3 -> 0, of which waited for: 3 -> 0; matrix products, arithmetic and copies ran while one was open for 6% -> 0% of each run, Pallas kernels for 10% -> 0%
where the time goes in v2:
time: 126 us; the launch traced here: 125 us
  Pallas kernels  124 us (98%)
  local copies, waits for them, and re-layouts  1.87 us (1%)
    pallas_call x1, Pallas kernels, fused(): pl.pallas_call(layer_kernel, out_shape=jax.ShapeDtypeStruct((rows, channe...  124 us

profile of v2, /device:TPU:13, one launch (start us, length us, event | category | flops | bytes accessed | tf_op | source)
XLA Modules:
  0.0 125.5 jit_solution(14245788479455844676)
XLA Ops:
  0.0 123.6 %shard_map.91 = bf16[256,1024]{1,0:T(8,128)(2,1)} custom-call(f32[4,9,8]{2,1,0:T(8,128)} %constant.6.clone.coef_ref, bf16[256,1024]{1,0:T(8,128)(2,1)} %q_ref.1, bf16[256,1024]{1,0:T(8,128)(2,1)} %k_ref.1, bf16[256,1024]{1,0:T(8,128)(2,1)} %v_ref.1, f32[256,1024]{1,0:T(8,128)} %f_ref.1, f32[1,1024]{1,0:T(1,128)} %bitcast.1, bf16[1024,512]{1,0:T(8,128)(2,1)} %w_ref.1, ...), custom_call_target="tpu_custom_call" | custom-call | tf_op jit(solution)/shard_map/pallas_call | solution.py:293
  123.6 1.9 %copy.11 = bf16[256,1024]{1,0:T(8,128)(2,1)} copy(bf16[256,1024]{1,0:T(8,128)(2,1)} %shard_map.91) | data formatting | bytes 1048576

commit v3 on v2

--- a/solution.py
+++ b/solution.py
@@ -165,15 +165,17 @@
     def _():
         local.start()
 
-    def start_weights():
+    def start_weights(distant):
         for dest, copy in weight:
-            @pl.when(dest != me)
+            near = ((dest // seq_t) // 2 == ib // 2) | (dest % seq_t == it)
+
+            @pl.when(jnp.logical_not(near) if distant else near & (dest != me))
             def _():
                 copy.start()
 
+    start_weights(False)
     for copy in entry:
         copy.wait_recv()
-    start_weights()
 
     acc_ref[...] = jnp.zeros_like(acc_ref)
 
@@ -213,6 +215,7 @@
         copy = remote(cs_send.at[j], cs_recv.at[me], back_s.at[j], back_r.at[j], place(d))
         copy.start()
         back.append(copy)
+    start_weights(True)
     cs_recv[me] = acc_ref[me].astype(jnp.bfloat16)
     for copy in back:
         copy.wait_recv()
@@ -238,30 +241,40 @@
         def _():
             local.wait()
 
-    def give(j):
-        c = (z + j) % depth
-        return remote(p_send.at[j], p_recv.at[j], p_s.at[j], p_r.at[j], {"ch": c})
+    def give(c):
+        return remote(p_send.at[c], p_recv.at[z], p_s.at[c], p_r.at[z], {"ch": c})
+
+    def take(c):
+        return remote(p_send.at[c], p_recv.at[c], p_s.at[c], p_r.at[c], {"ch": c})
 
     def project(j, carry):
-        c = (z + j) % depth
+        c = (ib // 2 * 2 + j) % depth
         weight_ready(c)
         for half in range(2):
             part = jnp.dot(g_ref[half], w_all[c], preferred_element_type=jnp.float32)
-            p_send[j, half] = part.astype(jnp.bfloat16)
-        give(j).start()
+
+            @pl.when(c == z)
+            def _():
+                p_own[half] = part
+
+            @pl.when(c != z)
+            def _():
+                p_send[c, half] = part.astype(jnp.bfloat16)
+
+        @pl.when(c != z)
+        def _():
+            give(c).start()
+
         return carry
 
-    lax.fori_loop(1, depth, project, 0)
-    weight_ready(z)
-    for half in range(2):
-        p_own[half] = jnp.dot(g_ref[half], w_all[z], preferred_element_type=jnp.float32)
+    lax.fori_loop(0, depth, project, 0)
     for j in range(1, depth):
-        give(j).wait_recv()
+        take((z + j) % depth).wait_recv()
 
     def total(half):
         s = p_own[half]
         for j in range(1, depth):
-            s += p_recv[j, half].astype(jnp.float32)
+            s += p_recv[(z + j) % depth, half].astype(jnp.float32)
         return s.astype(jnp.bfloat16)
 
     o_send[...] = total(1 - core)
@@ -278,7 +291,7 @@
         def _():
             copy.wait_send()
     for j in range(1, depth):
-        give(j).wait_send()
+        give((z + j) % depth).wait_send()
 
 
 def fused(query_gate, key_proj, value_proj, filters, skip_gain, w_out):

time: 126 us -> 104 us (0.83); the launches traced: 125 us -> 102 us
  Pallas kernels: 124 us -> 100 us
    pallas_call x1, Pallas kernels: 124 us -> 100 us  [fused(): pl.pallas_call(layer_kernel, out_shape=jax.ShapeDtypeStruct((rows, channe...]
where the time goes in v3:
time: 104 us; the launch traced here: 102 us
  Pallas kernels  100 us (96%)
  local copies, waits for them, and re-layouts  1.87 us (2%)
    pallas_call x1, Pallas kernels, fused(): pl.pallas_call(layer_kernel, out_shape=jax.ShapeDtypeStruct((rows, channe...  100 us

profile of v3, /device:TPU:13, one launch (start us, length us, event | category | flops | bytes accessed | tf_op | source)
XLA Modules:
  0.0 102.0 jit_solution(10312522079508108454)
XLA Ops:
  0.0 100.1 %shard_map.91 = bf16[256,1024]{1,0:T(8,128)(2,1)} custom-call(f32[4,9,8]{2,1,0:T(8,128)} %constant.6.clone.coef_ref, bf16[256,1024]{1,0:T(8,128)(2,1)} %q_ref.1, bf16[256,1024]{1,0:T(8,128)(2,1)} %k_ref.1, bf16[256,1024]{1,0:T(8,128)(2,1)} %v_ref.1, f32[256,1024]{1,0:T(8,128)} %f_ref.1, f32[1,1024]{1,0:T(1,128)} %bitcast.1, bf16[1024,512]{1,0:T(8,128)(2,1)} %w_ref.1, ...), custom_call_target="tpu_custom_call" | custom-call | tf_op jit(solution)/shard_map/pallas_call | solution.py:306
  100.1 1.9 %copy.11 = bf16[256,1024]{1,0:T(8,128)(2,1)} copy(bf16[256,1024]{1,0:T(8,128)(2,1)} %shard_map.91) | data formatting | bytes 1048576

commit v4 on v3

--- a/solution.py
+++ b/solution.py
@@ -105,7 +105,7 @@
 
 def layer_kernel(coef_ref, q_ref, k_ref, v_ref, f_ref, skip_ref, w_ref, base_ref, twid_ref, out_ref,
                  xs_send, xs_recv, acc_ref, cs_send, cs_recv, g_ref, w_all, p_send, p_recv, p_own,
-                 o_send, o_recv, in_s, in_r, back_s, back_r, w_s, w_r, g_s, g_r, p_s, p_r, o_s, o_r, local_sem):
+                 o_send, o_recv, in_s, in_r, back_s, back_r, w_s, w_r, g_s, g_r, p_s, p_r, o_s, o_r, local_sem, f_s, r_recv, p_far, r_r):
     seq_t = lax.axis_size("seqt")
     blocks = lax.axis_size("seqb") * seq_t
     depth = lax.axis_size("ch")
@@ -165,15 +165,15 @@
     def _():
         local.start()
 
-    def start_weights(distant):
+    def start_weights():
         for dest, copy in weight:
             near = ((dest // seq_t) // 2 == ib // 2) | (dest % seq_t == it)
 
-            @pl.when(jnp.logical_not(near) if distant else near & (dest != me))
+            @pl.when(near & (dest != me))
             def _():
                 copy.start()
 
-    start_weights(False)
+    start_weights()
     for copy in entry:
         copy.wait_recv()
 
@@ -215,7 +215,12 @@
         copy = remote(cs_send.at[j], cs_recv.at[me], back_s.at[j], back_r.at[j], place(d))
         copy.start()
         back.append(copy)
-    start_weights(True)
+    same = it == core
+    passed = jnp.where(same, (1 - ib // 2) * 2, ib // 2 * 2 + 1)
+    onward = {"seqb": jnp.where(same, ib, (ib + 2) % 4), "seqt": jnp.where(same, 1 - it, it)}
+    forward = remote(w_all.at[passed], w_all.at[passed], f_s, w_r.at[passed], onward)
+    forward.wait_recv()
+    forward.start()
     cs_recv[me] = acc_ref[me].astype(jnp.bfloat16)
     for copy in back:
         copy.wait_recv()
@@ -233,7 +238,7 @@
     def weight_ready(c):
         source = c * per + core
 
-        @pl.when(source != me)
+        @pl.when((source != me) & (c != passed))
         def _():
             remote(w_ref, w_all.at[c], w_s.at[0], w_r.at[c], sibling).wait_recv()
 
@@ -247,35 +252,71 @@
     def take(c):
         return remote(p_send.at[c], p_recv.at[c], p_s.at[c], p_r.at[c], {"ch": c})
 
-    def project(j, carry):
-        c = (ib // 2 * 2 + j) % depth
-        weight_ready(c)
+    beside = z + 1 - 2 * (z % 2)
+    outer = (z == 0) | (z == 3)
+    inner = jnp.logical_not(outer)
+    far = [jnp.where(z < 2, 3 - i, i) for i in range(2)]
+    relay = [
+        remote(p_send.at[far[i]], r_recv.at[i], p_s.at[far[i]], r_r.at[i], {"ch": beside})
+        for i in range(2)
+    ]
+
+    def partial(c, half):
+        return jnp.dot(g_ref[half], w_all[c], preferred_element_type=jnp.float32)
+
+    for i in range(2):
+        weight_ready(far[i])
         for half in range(2):
-            part = jnp.dot(g_ref[half], w_all[c], preferred_element_type=jnp.float32)
-
-            @pl.when(c == z)
+            part = partial(far[i], half)
+
+            @pl.when(outer)
             def _():
-                p_own[half] = part
-
-            @pl.when(c != z)
+                p_send[far[i], half] = part.astype(jnp.bfloat16)
+
+            @pl.when(inner)
             def _():
-                p_send[c, half] = part.astype(jnp.bfloat16)
-
-        @pl.when(c != z)
+                p_far[i, half] = part
+
+        @pl.when(outer)
         def _():
-            give(c).start()
-
-        return carry
-
-    lax.fori_loop(0, depth, project, 0)
-    for j in range(1, depth):
-        take((z + j) % depth).wait_recv()
+            if i:
+                relay[0].wait_send()
+            relay[i].start()
+
+    weight_ready(beside)
+    for half in range(2):
+        p_send[beside, half] = partial(beside, half).astype(jnp.bfloat16)
+
+    @pl.when(inner)
+    def _():
+        give(beside).start()
+
+    weight_ready(z)
+    for half in range(2):
+        p_own[half] = partial(z, half)
+
+    @pl.when(outer)
+    def _():
+        relay[1].wait_send()
+        give(beside).start()
+
+    @pl.when(inner)
+    def _():
+        for i in range(2):
+            relay[i].wait_recv()
+            for half in range(2):
+                p_send[far[i], half] = (
+                    p_far[i, half] + r_recv[i, half].astype(jnp.float32)
+                ).astype(jnp.bfloat16)
+            give(far[i]).start()
+
+    across = jnp.where(z < 2, 2, 1)
+    take(across).wait_recv()
+    take(beside).wait_recv()
 
     def total(half):
-        s = p_own[half]
-        for j in range(1, depth):
-            s += p_recv[(z + j) % depth, half].astype(jnp.float32)
-        return s.astype(jnp.bfloat16)
+        s = p_own[half] + p_recv[beside, half].astype(jnp.float32)
+        return (s + p_recv[across, half].astype(jnp.float32)).astype(jnp.bfloat16)
 
     o_send[...] = total(1 - core)
     last = remote(o_send, o_recv, o_s, o_r, sibling)
@@ -287,11 +328,18 @@
     for copy in entry + back:
         copy.wait_send()
     for dest, copy in weight:
-        @pl.when(dest != me)
+        near = ((dest // seq_t) // 2 == ib // 2) | (dest % seq_t == it)
+
+        @pl.when(near & (dest != me))
         def _():
             copy.wait_send()
-    for j in range(1, depth):
-        give((z + j) % depth).wait_send()
+    forward.wait_send()
+    give(beside).wait_send()
+
+    @pl.when(inner)
+    def _():
+        for i in range(2):
+            give(far[i]).wait_send()
 
 
 def fused(query_gate, key_proj, value_proj, filters, skip_gain, w_out):
@@ -323,7 +371,8 @@
             pltpu.VMEM((rows, cols), bf16),
             dma((blocks,)), dma((blocks,)), dma((blocks,)), dma((blocks,)),
             dma((blocks // 2,)), dma((depth,)),
-            dma, dma, dma((depth,)), dma((depth,)), dma, dma, dma,
+            dma, dma, dma((depth,)), dma((depth,)), dma, dma, dma, dma,
+            pltpu.VMEM((2, 2, rows, cols), bf16), pltpu.VMEM((2, 2, rows, cols), f32), dma((2,)),
         ],
         compiler_params=pltpu.CompilerParams(
             collective_id=0, has_side_effects=True, vmem_limit_bytes=56 * 1024 * 1024
@@ -336,7 +385,7 @@
     rows, channels = key_proj.shape
     seq = lax.axis_size(SEQ)
     width = channels // seq
-    if width % 128 == 0 and seq == 2 * lax.axis_size("ch") and lax.axis_size("seqb") % 2 == 0:
+    if width % 128 == 0 and seq == 2 * lax.axis_size("ch") and lax.axis_size("seqb") == 4 and lax.axis_size("ch") == 4:
         return fused(query_gate, key_proj, value_proj, filters, skip_gain, w_out)
     product = key_proj.astype(jnp.float32) * value_proj.astype(jnp.float32)
     pieces = lambda a: a.astype(jnp.bfloat16).reshape(rows, seq, width).transpose(1, 0, 2)

time: 104 us -> 94.2 us (0.906)
  Pallas kernels: 100 us -> 91 us
    pallas_call x1, Pallas kernels: 100 us -> 91 us  [fused(): pl.pallas_call(layer_kernel, out_shape=jax.ShapeDtypeStruct((rows, channe...]
where the time goes in v4:
time: 94.2 us; the launch traced here: 92.8 us
  Pallas kernels  91 us (97%)
  local copies, waits for them, and re-layouts  1.87 us (2%)
    pallas_call x1, Pallas kernels, fused(): pl.pallas_call(layer_kernel, out_shape=jax.ShapeDtypeStruct((rows, channe...  91 us

profile of v4, /device:TPU:13, one launch (start us, length us, event | category | flops | bytes accessed | tf_op | source)
XLA Modules:
  0.0 92.8 jit_solution(14435246126869694298)
XLA Ops:
  0.0 91.0 %shard_map.91 = bf16[256,1024]{1,0:T(8,128)(2,1)} custom-call(f32[4,9,8]{2,1,0:T(8,128)} %constant.6.clone.coef_ref, bf16[256,1024]{1,0:T(8,128)(2,1)} %q_ref.1, bf16[256,1024]{1,0:T(8,128)(2,1)} %k_ref.1, bf16[256,1024]{1,0:T(8,128)(2,1)} %v_ref.1, f32[256,1024]{1,0:T(8,128)} %f_ref.1, f32[1,1024]{1,0:T(1,128)} %bitcast.1, bf16[1024,512]{1,0:T(8,128)(2,1)} %w_ref.1, ...), custom_call_target="tpu_custom_call" | custom-call | tf_op jit(solution)/shard_map/pallas_call | solution.py:354
  91.0 1.9 %copy.11 = bf16[256,1024]{1,0:T(8,128)(2,1)} copy(bf16[256,1024]{1,0:T(8,128)(2,1)} %shard_map.91) | data formatting | bytes 1048576
